TPU v7x, 32 devices: a whole 2x2x4 slice. The times are simulated.
32 devices in a mesh: groups: 2 (over x), ctx: 16 (over z, y, core).
Axes of the slice: x: 2, y: 2, z: 4, core: 2. Of those that a mesh axis runs over, the one named last changes fastest.
Arguments:
- context_keys: bfloat16 [4096, 2048], P(('groups', 'ctx')), parts along dimension 0, may hold values from -6 to 6
- context_values: bfloat16 [4096, 2048], P(('groups', 'ctx')), parts along dimension 0, may hold values from -6 to 6
- context_queries: bfloat16 [4096, 2048], P(('groups', 'ctx')), parts along dimension 0, may hold values from -6 to 6
- token_rates: float32 [8, 4096], P(None, ('groups', 'ctx')), parts along dimension 1, may hold values from 0.05 to 1
- w_gate: bfloat16 [8, 256, 256], replicated, may hold values from -0.375 to 0.375
- w_up: bfloat16 [8, 256, 256], replicated, may hold values from -0.375 to 0.375
- w_down: bfloat16 [8, 256, 256], replicated, may hold values from -0.375 to 0.375
- question_rows: bfloat16 [8192, 2048], P(('groups', 'ctx')), parts along dimension 0, may hold values from -6 to 6
- question_count: int32 [32], P(('groups', 'ctx')), parts along dimension 0, may hold values from 1 to 256, 1024 in all
Outputs:
- context_out: bfloat16 [4096, 2048], P(('groups', 'ctx')), parts along dimension 0
- answers: bfloat16 [8192, 2048], P(('groups', 'ctx')), parts along dimension 0
There are 2 independent parts, one for each index of `groups`. A program takes and returns all parts, laid end to end along the dimension named above; an argument that names none is the same for every part. Nothing has to cross between parts.
Inputs may be any that keep to these rules, and one draw needn't show every extreme that they name: `question_count`: live rows are the first of each device's 256 slots. The counts of one user (the devices along ctx) add up to exactly 1024, and some device of each user has exactly 256.
All inputs are finite; a program needn't handle non-finite values.
Results may differ from a plain program's by a relative error of at most 0.018.
Values may be sent and summed in bfloat16 or wider, within the bound.
A program may use at most 128 MiB of HBM per device.

v0:
```python
import jax
import jax.numpy as jnp
from jax import lax
from jax.sharding import PartitionSpec as P

NS_STEPS = 3
quintic_first = 3.4445
quintic_second = -4.775
quintic_third = 2.0315


def fast_apply(in_rows, w_gate, w_up, w_down):
    head_count = w_gate.shape[0]
    head_size = w_gate.shape[1]
    row_split = in_rows.reshape(in_rows.shape[0], head_count, head_size)
    pre_gate = jnp.einsum("thd,hde->hte", row_split, w_gate, preferred_element_type=jnp.float32)
    pre_up = jnp.einsum("thd,hde->hte", row_split, w_up, preferred_element_type=jnp.float32)
    hidden = (jax.nn.silu(pre_gate) * pre_up).astype(jnp.bfloat16)
    outputs = jnp.einsum("hte,hef->thf", hidden, w_down, preferred_element_type=jnp.float32)
    return outputs.reshape(in_rows.shape[0], head_count * head_size).astype(jnp.bfloat16)


def directions(context_keys, context_values, token_rates, w_gate, w_up, w_down):
    tok_rows = context_keys.shape[0]
    head_count = w_gate.shape[0]
    head_size = w_gate.shape[1]
    key_split = context_keys.reshape(tok_rows, head_count, head_size)
    value_split = context_values.reshape(tok_rows, head_count, head_size)
    pre_gate = jnp.einsum("thd,hde->hte", key_split, w_gate, preferred_element_type=jnp.float32)
    pre_up = jnp.einsum("thd,hde->hte", key_split, w_up, preferred_element_type=jnp.float32)
    sigmoid_gate = jax.nn.sigmoid(pre_gate)
    activated = pre_gate * sigmoid_gate
    hidden = (activated * pre_up).astype(jnp.bfloat16)
    weighted = (token_rates.T[:, :, None] * value_split).astype(jnp.bfloat16)
    back_hidden = jnp.einsum("thf,hef->hte", weighted, w_down, preferred_element_type=jnp.float32)
    back_gate = (
        back_hidden * pre_up * sigmoid_gate * (1.0 + pre_gate * (1.0 - sigmoid_gate))
    ).astype(jnp.bfloat16)
    back_up = (back_hidden * activated).astype(jnp.bfloat16)
    step_gate = jnp.einsum("thd,hte->hde", key_split, back_gate, preferred_element_type=jnp.float32)
    step_up = jnp.einsum("thd,hte->hde", key_split, back_up, preferred_element_type=jnp.float32)
    step_down = jnp.einsum("hte,thf->hef", hidden, weighted, preferred_element_type=jnp.float32)
    return jnp.stack([step_gate, step_up, step_down])


def per_device(
    context_keys,
    context_values,
    context_queries,
    token_rates,
    w_gate,
    w_up,
    w_down,
    question_rows,
    question_count,
):
    head_count = w_gate.shape[0]
    head_size = w_gate.shape[1]
    matrix_count = 3 * head_count
    context_out = fast_apply(context_queries, w_gate, w_up, w_down)
    direction = directions(context_keys, context_values, token_rates, w_gate, w_up, w_down)
    flat_grads = direction.reshape(matrix_count, head_size * head_size)
    total = lax.psum(flat_grads, "ctx")
    norm_sizes = jnp.sqrt(jnp.sum(total * total, axis=1, keepdims=True))
    scaled = (total / (norm_sizes + 1e-06)).astype(jnp.bfloat16)
    iterate = scaled.reshape(matrix_count, head_size, head_size)
    for sweep_index in range(NS_STEPS):
        gram_matrix = jnp.einsum(
            "mij,mkj->mik", iterate, iterate, preferred_element_type=jnp.float32
        ).astype(jnp.bfloat16)
        gram_square = jnp.einsum(
            "mij,mjk->mik", gram_matrix, gram_matrix, preferred_element_type=jnp.float32
        )
        polynomial = (
            quintic_second * gram_matrix.astype(jnp.float32) + quintic_third * gram_square
        ).astype(jnp.bfloat16)
        product = jnp.einsum(
            "mij,mjk->mik", polynomial, iterate, preferred_element_type=jnp.float32
        )
        iterate = (quintic_first * iterate.astype(jnp.float32) + product).astype(jnp.bfloat16)
    previous = jnp.stack([w_gate, w_up, w_down]).astype(jnp.float32)
    moved = previous + iterate.reshape(3, head_count, head_size, head_size).astype(jnp.float32)
    col_norms = jnp.sqrt(jnp.sum(previous * previous, axis=2, keepdims=True))
    updated = (
        moved * col_norms / jnp.sqrt(jnp.sum(moved * moved, axis=2, keepdims=True) + 1e-06)
    ).astype(jnp.bfloat16)
    capacity = question_rows.shape[0]
    outputs = fast_apply(question_rows, updated[0], updated[1], updated[2])
    live_mask = jnp.arange(capacity, dtype=jnp.int32) < question_count[0]
    answers = jnp.where(live_mask[:, None], outputs, jnp.zeros_like(outputs))
    return (context_out, answers)


def solution(mesh):
    return jax.shard_map(
        per_device,
        mesh=mesh,
        in_specs=(
            P(("groups", "ctx"), None),
            P(("groups", "ctx"), None),
            P(("groups", "ctx"), None),
            P(None, ("groups", "ctx")),
            P(),
            P(),
            P(),
            P(("groups", "ctx"), None),
            P(("groups", "ctx")),
        ),
        out_specs=(P(("groups", "ctx"), None), P(("groups", "ctx"), None)),
        check_vma=False,
    )
```

profile of v0, /device:TPU:0, one launch (start us, length us, event | category | flops | bytes accessed | tf_op | source)
XLA Modules:
  0.0 236.1 jit_solution(8442899116746412055)
XLA Ops:
  7.3 1.8 fusion.41
  9.1 1.4 fusion.43
  13.4 3.3 %pad_maximum_fusion = f32[3,8,256,256]{2,3,1,0:T(8,128)} fusion(f32[1,8,256,256]{2,3,1,0:T(8,128)S(1)} %convolution_bitcast_fusion, f32[1,8,256,256]{2,3,1,0:T(8,128)S(1)} %convolution_bitcast_fusion.1, f32[1,8,256,256]{2,3,1,0:T(8,128)S(1)} %convolution_bitcast_fusion.2), kind=kLoop, calls=%fused_computation | loop fusion | flops 3145728 | bytes 12582912 | tf_op jit(solution)/shard_map/stack | solution.py:43
  16.7 6.7 %copy.60 = f32[3,8,256,256]{3,1,2,0:T(8,128)} copy(f32[3,8,256,256]{2,3,1,0:T(8,128)} %pad_maximum_fusion) | data formatting | bytes 12582912
  25.7 1.9 copy.33
  27.5 3.1 %maximum_convert_fusion = f32[3,8,256,256]{2,3,1,0:T(8,128)} fusion(bf16[1,8,256,256]{2,3,1,0:T(8,128)(2,1)S(1)} %bitcast.124, bf16[1,8,256,256]{2,3,1,0:T(8,128)(2,1)S(1)} %bitcast.121, bf16[1,8,256,256]{2,3,1,0:T(8,128)(2,1)S(1)} %bitcast.118), kind=kLoop, calls=%fused_computation.18 | loop fusion | flops 4718592 | bytes 9437184 | tf_op jit(solution)/shard_map/convert_element_type | solution.py:81
  30.6 7.0 %copy.45 = f32[3,8,256,256]{3,2,1,0:T(8,128)} copy(f32[3,8,256,256]{2,3,1,0:T(8,128)} %maximum_convert_fusion) | data formatting | bytes 12582912 | tf_op jit(solution)/shard_map/convert_element_type | solution.py:81
  38.6 2.4 %copy.56 = bf16[256,2048]{0,1:T(8,128)(2,1)} copy(bf16[256,2048]{1,0:T(8,128)(2,1)} %param.16) | data formatting | bytes 2097152 | tf_op jit(solution)/shard_map/reshape | solution.py:15
  41.7 1.7 fusion.47
  43.4 2.5 %fusion.29 = bf16[128,8,256]{2,0,1:T(8,128)(2,1)} fusion(bf16[8,256,256]{2,1,0:T(8,128)(2,1)S(1)} %copy-done.10, bf16[8,256,256]{2,1,0:T(8,128)(2,1)S(1)} %copy-done.12, f32[8,128,256]{2,1,0:T(8,128)S(1)} %fusion.47, bf16[16,8,8,256]{3,2,1,0:T(8,128)(2,1)} %bitcast.140), kind=kOutput, calls=%fused_computation.45 | convolution fusion | flops 270270464 | bytes 4194304 | tf_op jit(solution)/shard_map/hte,hef->thf/dot_general | solution.py:19
  45.9 1.3 copy.30
  48.3 117.3 %all-reduce.2.cloned.1.call-done = f32[24,65536]{1,0:T(8,128)} async-done(((f32[24,65536]{1,0:T(8,128)}), f32[24,65536]{1,0:T(8,128)}) %all-reduce.2.cloned.1.call-update) | async-done | bytes 6291472 | tf_op jit(solution)/shard_map/psum | solution.py:63
  165.5 3.6 %multiply_reduce_fusion.1 = f32[24]{0:T(128)S(1)} fusion(f32[24,65536]{1,0:T(8,128)} %all-reduce.2.cloned.1.call-done), kind=kLoop, calls=%fused_computation.13 | loop fusion | flops 3145704 | bytes 6291552 | tf_op jit(solution)/shard_map/reduce_sum | solution.py:64
  171.3 2.7 %fusion.74 = bf16[24,256,256]{2,1,0:T(8,128)(2,1)} fusion(bf16[24,256,256]{2,1,0:T(8,128)(2,1)S(1)} %bitcast.115), kind=kOutput, calls=%fused_computation.96 | convolution fusion | flops 805306368 | bytes 6291456 | tf_op jit(solution)/shard_map/mij,mkj->mik/dot_general | solution.py:68
  173.9 7.8 %add_convert_fusion.4 = bf16[24,256,256]{2,1,0:T(8,128)(2,1)} fusion(bf16[24,256,256]{2,1,0:T(8,128)(2,1)S(1)} %bitcast.116, bf16[24,256,256]{2,1,0:T(8,128)(2,1)} %fusion.74), kind=kOutput, calls=%fused_computation.10 | convolution fusion | flops 1624768512 | bytes 9437184 | tf_op jit(solution)/shard_map/mij,mjk->mik/dot_general | solution.py:77
  181.8 5.5 %fusion.75 = bf16[24,256,256]{2,1,0:T(8,128)(2,1)} fusion(bf16[24,256,256]{2,1,0:T(8,128)(2,1)} %add_convert_fusion.4), kind=kOutput, calls=%fused_computation.97 | convolution fusion | flops 805306368 | bytes 6291456 | tf_op jit(solution)/shard_map/mij,mkj->mik/dot_general | solution.py:68
  187.3 8.2 %add_convert_fusion.2 = bf16[24,256,256]{2,1,0:T(8,128)(2,1)S(1)} fusion(bf16[24,256,256]{2,1,0:T(8,128)(2,1)} %add_convert_fusion.4, bf16[24,256,256]{2,1,0:T(8,128)(2,1)} %fusion.75), kind=kOutput, calls=%fused_computation.8 | convolution fusion | flops 1624768512 | bytes 9437184 | tf_op jit(solution)/shard_map/mij,mjk->mik/dot_general | solution.py:77
  195.5 2.7 %fusion.76 = bf16[24,256,256]{2,1,0:T(8,128)(2,1)} fusion(bf16[24,256,256]{2,1,0:T(8,128)(2,1)S(1)} %add_convert_fusion.2), kind=kOutput, calls=%fused_computation.98 | convolution fusion | flops 805306368 | bytes 6291456 | tf_op jit(solution)/shard_map/mij,mkj->mik/dot_general | solution.py:68
  198.1 11.6 %fusion.1 = (f32[24,256]{1,0:T(8,128)S(1)}, f32[24,256,256]{2,1,0:T(8,128)}) fusion(f32[3,8,256,256]{3,2,1,0:T(8,128)} %copy.45, bf16[24,256,256]{2,1,0:T(8,128)(2,1)S(1)} %add_convert_fusion.2, bf16[24,256,256]{2,1,0:T(8,128)(2,1)} %fusion.76), kind=kOutput, calls=%fused_computation.3 | convolution fusion | flops 1631053824 | bytes 18898944 | tf_op jit(solution)/shard_map/mij,mjk->mik/dot_general | solution.py:77
  209.7 6.7 %copy.44 = f32[3,8,256,256]{2,3,1,0:T(8,128)} copy(f32[3,8,256,256]{3,2,1,0:T(8,128)} %bitcast.128) | data formatting | bytes 12582912 | tf_op jit(solution)/shard_map/convert_element_type | solution.py:82
  216.5 4.6 %divide_convert_fusion = bf16[3,8,256,256]{2,3,1,0:T(8,128)(2,1)S(1)} fusion(f32[3,8,256,256]{2,3,1,0:T(8,128)} %copy.44, f32[3,8,256]{2,1,0:T(8,128)S(1)} %sqrt_bitcast_fusion, f32[3,8,256]{2,1,0:T(8,128)S(1)} %sqrt.28, bf16[1,8,256,256]{2,3,1,0:T(8,128)(2,1)S(1)} %bitcast.126, bf16[1,8,256,256]{2,3,1,0:T(8,128)(2,1)S(1)} %bitcast.123, ...), kind=kLoop, calls=%fused_computation.4 | loop fusion | flops 11010048 | bytes 12632064 | tf_op jit(solution)/shard_map/convert_element_type | solution.py:86
  221.1 1.6 copy-done.8
  223.1 3.5 %convolution_convert_fusion = bf16[8,256,256]{2,1,0:T(8,128)(2,1)} fusion(f32[8,256,256]{2,1,0:T(8,128)S(1)} %fusion.31, bf16[256,8,256]{0,2,1:T(8,128)(2,1)S(1)} %bitcast.132, bf16[3,8,256,256]{2,3,1,0:T(8,128)(2,1)} %copy-done.8), kind=kOutput, calls=%fused_computation.41 | convolution fusion | flops 540540928 | bytes 6291456 | tf_op jit(solution)/shard_map/hte,hef->thf/dot_general | solution.py:19
  226.7 1.5 copy.48
  (54 shorter events, 10.9 us)
Async XLA Ops:
  7.2 1.9 copy-start.11
  7.2 3.3 %copy-start.16 = (bf16[128,2048]{1,0:T(8,128)(2,1)S(1)}, bf16[128,2048]{1,0:T(8,128)(2,1)}, u32[]{:S(2)}) copy-start(bf16[128,2048]{1,0:T(8,128)(2,1)} %param.10) | copy-start | bytes 1572868
  7.2 158.3 %all-reduce.2.cloned.1.call-start = ((), (), s32[]{:S(2)}) async-start(), calls=%async_computation | async-start | bytes 12582912 | tf_op jit(solution)/shard_map/psum | solution.py:63
  7.2 3.4 %copy-start.9 = (bf16[8,256,256]{2,1,0:T(8,128)(2,1)S(1)}, bf16[8,256,256]{2,1,0:T(8,128)(2,1)}, u32[]{:S(2)}) copy-start(bf16[8,256,256]{2,1,0:T(8,128)(2,1)} %param.15) | copy-start | bytes 3145732
  7.2 3.3 %copy-start.17 = (f32[8,128]{1,0:T(8,128)S(1)}, f32[8,128]{1,0:T(8,128)}, u32[]{:S(2)}) copy-start(f32[8,128]{1,0:T(8,128)} %param.12) | copy-start | bytes 12292
  11.1 1.0 copy-start.15
  23.4 1.2 copy-start.7
  25.1 12.5 %copy-start.1 = (bf16[8,256,256]{1,2,0:T(8,128)(2,1)}, bf16[8,256,256]{1,2,0:T(8,128)(2,1)S(1)}, u32[]{:S(2)}) copy-start(bf16[8,256,256]{1,2,0:T(8,128)(2,1)S(1)} %copy.31) | copy-start | bytes 3145732
  25.6 11.9 %copy-start.3 = (bf16[8,256,256]{1,2,0:T(8,128)(2,1)}, bf16[8,256,256]{1,2,0:T(8,128)(2,1)S(1)}, u32[]{:S(2)}) copy-start(bf16[8,256,256]{1,2,0:T(8,128)(2,1)S(1)} %copy.32) | copy-start | bytes 3145732
  27.5 10.1 %copy-start.5 = (bf16[8,256,256]{1,2,0:T(8,128)(2,1)}, bf16[8,256,256]{1,2,0:T(8,128)(2,1)S(1)}, u32[]{:S(2)}) copy-start(bf16[8,256,256]{1,2,0:T(8,128)(2,1)S(1)} %copy.33) | copy-start | bytes 3145732
  38.6 4.8 %copy-start.10 = (bf16[8,256,256]{2,1,0:T(8,128)(2,1)S(1)}, bf16[8,256,256]{2,1,0:T(8,128)(2,1)}, u32[]{:S(2)}) copy-start(bf16[8,256,256]{2,1,0:T(8,128)(2,1)} %param.15) | copy-start | bytes 3145732
  38.6 4.8 %copy-start.12 = (bf16[8,256,256]{2,1,0:T(8,128)(2,1)S(1)}, bf16[8,256,256]{2,1,0:T(8,128)(2,1)}, u32[]{:S(2)}) copy-start(bf16[8,256,256]{2,1,0:T(8,128)(2,1)} %param.14) | copy-start | bytes 3145732
  165.5 4.6 %copy-start = (f32[24,65536]{1,0:T(8,128)S(1)}, f32[24,65536]{1,0:T(8,128)}, u32[]{:S(2)}) copy-start(f32[24,65536]{1,0:T(8,128)} %all-reduce.2.cloned.1.call-done) | copy-start | bytes 18874372
  209.7 6.7 %copy-start.2 = (bf16[8,256,256]{1,2,0:T(8,128)(2,1)S(1)}, bf16[8,256,256]{1,2,0:T(8,128)(2,1)}, u32[]{:S(2)}) copy-start(bf16[8,256,256]{1,2,0:T(8,128)(2,1)} %copy-done.1) | copy-start | bytes 3145732
  209.7 6.7 %copy-start.4 = (bf16[8,256,256]{1,2,0:T(8,128)(2,1)S(1)}, bf16[8,256,256]{1,2,0:T(8,128)(2,1)}, u32[]{:S(2)}) copy-start(bf16[8,256,256]{1,2,0:T(8,128)(2,1)} %copy-done.3) | copy-start | bytes 3145732
  209.7 6.7 %copy-start.6 = (bf16[8,256,256]{1,2,0:T(8,128)(2,1)S(1)}, bf16[8,256,256]{1,2,0:T(8,128)(2,1)}, u32[]{:S(2)}) copy-start(bf16[8,256,256]{1,2,0:T(8,128)(2,1)} %copy-done.5) | copy-start | bytes 3145732
  216.5 6.2 %copy-start.13 = (bf16[256,2048]{0,1:T(8,128)(2,1)S(1)}, bf16[256,2048]{0,1:T(8,128)(2,1)}, u32[]{:S(2)}) copy-start(bf16[256,2048]{0,1:T(8,128)(2,1)} %copy.56) | copy-start | bytes 3145732
  221.1 1.6 copy-start.8
  221.1 2.1 copy-start.14
Sparse Core Ops, SparseCore 0:
  23.5 141.9 all-reduce.1
where the time goes:
time: 237 us; the launch traced here: 236 us
  waiting for transfers between devices  117 us (49%)
  matrix products  52.2 us (22%)
  local copies, waits for them, and re-layouts  34.4 us (15%)
  other arithmetic  17.2 us (7%)
  between operations  15 us (6%)
    psum x1, waiting for transfers between devices, per_device(): total = lax.psum(flat_grads, 'ctx')  117 us
    dot_general x3, matrix products, per_device(): jnp.einsum('mij,mjk->mik', polynomial, iterate, preferred_element_type=jn...  27.6 us
    unnamed x42, local copies, waits for them, and re-layouts  15.6 us
    dot_general x3, matrix products, per_device(): jnp.einsum('mij,mkj->mik', iterate, iterate, preferred_element_type=jnp.f...  10.9 us
    convert_element_type x1, local copies, waits for them, and re-layouts, per_device(): previous = jnp.stack([w_gate, w_up, w_down]).astype(jnp.float32)  6.96 us
    convert_element_type x1, local copies, waits for them, and re-layouts, per_device(): iterate.reshape(3, head_count, head_size, head_size).astype(jnp.float32)  6.7 us
    dot_general x2, matrix products, fast_apply(): jnp.einsum('hte,hef->thf', hidden, w_down, preferred_element_type=jnp.flo...  6.01 us
  transfers between devices with their start and end apart: 1, of which 1 were waited for; matrix products, arithmetic and copies ran while one was open for 10% of the time, Pallas kernels for 0%

commit v1 on v0

--- a/solution.py
+++ b/solution.py
@@ -60,7 +60,7 @@
     context_out = fast_apply(context_queries, w_gate, w_up, w_down)
     direction = directions(context_keys, context_values, token_rates, w_gate, w_up, w_down)
     flat_grads = direction.reshape(matrix_count, head_size * head_size)
-    total = lax.psum(flat_grads, "ctx")
+    total = jnp.sum(lax.all_gather(flat_grads, "ctx"), axis=0)
     norm_sizes = jnp.sqrt(jnp.sum(total * total, axis=1, keepdims=True))
     scaled = (total / (norm_sizes + 1e-06)).astype(jnp.bfloat16)
     iterate = scaled.reshape(matrix_count, head_size, head_size)

time: 237 us -> 623 us (2.63)
  waiting for transfers between devices: 117 us -> 467 us
  other arithmetic: 17.2 us -> 51.7 us
    all_gather x0 -> x1, waiting for transfers between devices: none -> 467 us  [per_device(): total = jnp.sum(lax.all_gather(flat_grads, 'ctx'), axis=0)]
    psum x1 -> x0, waiting for transfers between devices: 117 us -> none  [per_device(): total = lax.psum(flat_grads, 'ctx')]
    reduce_sum x0 -> x1, other arithmetic: none -> 33.5 us  [per_device(): total = jnp.sum(lax.all_gather(flat_grads, 'ctx'), axis=0)]
    another operation x0 -> x2, local copies, waits for them, and re-layouts: none -> 13.4 us  [the longest x1 6.83 us: per_device(): total = jnp.sum(lax.all_gather(flat_grads, 'ctx'), axis=0)]
    unnamed x42 -> x39, local copies, waits for them, and re-layouts: 15.6 us -> 10.2 us
  transfers between devices with their start and end apart: 1 -> 1, of which waited for: 1 -> 1; matrix products, arithmetic and copies ran while one was open for 10% -> 3% of each run, Pallas kernels for 0% -> 0%
where the time goes in v1:
time: 623 us; the launch traced here: 622 us
  waiting for transfers between devices  467 us (75%)
  other arithmetic  51.7 us (8%)
  matrix products  50.2 us (8%)
  local copies, waits for them, and re-layouts  38.4 us (6%)
  between operations  15 us (2%)
    all_gather x1, waiting for transfers between devices, per_device(): total = jnp.sum(lax.all_gather(flat_grads, 'ctx'), axis=0)  467 us
    reduce_sum x1, other arithmetic, per_device(): total = jnp.sum(lax.all_gather(flat_grads, 'ctx'), axis=0)  33.5 us
    dot_general x3, matrix products, per_device(): jnp.einsum('mij,mjk->mik', polynomial, iterate, preferred_element_type=jn...  27.5 us
  transfers between devices with their start and end apart: 1, of which 1 were waited for; matrix products, arithmetic and copies ran while one was open for 3% of the time, Pallas kernels for 0%

profile of v1, /device:TPU:0, one launch (start us, length us, event | category | flops | bytes accessed | tf_op | source)
XLA Modules:
  0.0 622.2 jit_solution(4624900573798227612)
XLA Ops:
  7.3 1.8 fusion.48
  9.1 1.4 fusion.50
  13.4 3.3 pad_maximum_fusion
  16.7 6.5 %copy.65 = f32[3,8,256,256]{3,2,1,0:T(8,128)} copy(f32[3,8,256,256]{2,3,1,0:T(8,128)} %pad_maximum_fusion) | data formatting | bytes 12582912 | tf_op jit(solution)/shard_map/stack | solution.py:43
  23.2 6.8 %all_gather_reshape.3 = f32[1,24,65536]{2,1,0:T(8,128)} reshape(f32[3,8,256,256]{3,2,1,0:T(8,128)} %copy.65) | data formatting | bytes 12582912 | tf_op jit(solution)/shard_map/all_gather;reshape | solution.py:63
  32.3 1.9 copy.55
  34.2 3.0 maximum_convert_fusion
  37.3 7.1 %copy.67 = f32[3,8,256,256]{3,2,1,0:T(8,128)} copy(f32[3,8,256,256]{2,3,1,0:T(8,128)} %maximum_convert_fusion) | data formatting | bytes 12582912 | tf_op jit(solution)/shard_map/convert_element_type | solution.py:81
  46.4 2.5 fusion.30
  50.2 466.9 %all-gather.2.cloned.1.call-done = f32[16,24,65536]{2,1,0:T(8,128)} async-done(((f32[1,24,65536]{2,1,0:T(8,128)}), f32[16,24,65536]{2,1,0:T(8,128)}) %all-gather.2.cloned.1.call-update) | async-done | bytes 100663312 | tf_op jit(solution)/shard_map/all_gather | solution.py:63
  517.1 33.5 %reduce_sum.38 = f32[24,65536]{1,0:T(8,128)} reduce(f32[16,24,65536]{2,1,0:T(8,128)} %all-gather.2.cloned.1.call-done, f32[]{:T(128)} %constant.8.clone.1), dimensions={0}, to_apply=%region_0.1 | reduce | flops 23592960 | bytes 106954752 | tf_op jit(solution)/shard_map/reduce_sum | solution.py:63
  550.6 3.6 multiply_reduce_fusion.1
  555.1 2.0 copy.82
  557.2 1.3 fusion
  558.5 2.7 fusion.81
  561.2 8.0 %add_convert_fusion.4 = bf16[24,256,256]{2,1,0:T(8,128)(2,1)} fusion(bf16[24,256,256]{2,1,0:T(8,128)(2,1)S(1)} %fusion, bf16[24,256,256]{2,1,0:T(8,128)(2,1)} %fusion.81), kind=kOutput, calls=%fused_computation.12 | convolution fusion | flops 1624768512 | bytes 9437184 | tf_op jit(solution)/shard_map/mij,mjk->mik/dot_general | solution.py:77
  569.3 5.5 fusion.82
  574.8 8.0 %add_convert_fusion.2 = bf16[24,256,256]{2,1,0:T(8,128)(2,1)S(1)} fusion(bf16[24,256,256]{2,1,0:T(8,128)(2,1)} %add_convert_fusion.4, bf16[24,256,256]{2,1,0:T(8,128)(2,1)} %fusion.82), kind=kOutput, calls=%fused_computation.10 | convolution fusion | flops 1624768512 | bytes 9437184 | tf_op jit(solution)/shard_map/mij,mjk->mik/dot_general | solution.py:77
  582.8 2.7 fusion.83
  585.6 11.4 %fusion.2 = (f32[24,256]{1,0:T(8,128)S(1)}, f32[24,256,256]{2,1,0:T(8,128)}) fusion(f32[3,8,256,256]{3,2,1,0:T(8,128)} %copy.67, bf16[24,256,256]{2,1,0:T(8,128)(2,1)S(1)} %add_convert_fusion.2, bf16[24,256,256]{2,1,0:T(8,128)(2,1)} %fusion.83), kind=kOutput, calls=%fused_computation.5 | convolution fusion | flops 1631053824 | bytes 18898944 | tf_op jit(solution)/shard_map/mij,mjk->mik/dot_general | solution.py:77
  597.0 6.7 %copy.66 = f32[3,8,256,256]{2,3,1,0:T(8,128)} copy(f32[3,8,256,256]{3,2,1,0:T(8,128)} %bitcast.131) | data formatting | bytes 12582912 | tf_op jit(solution)/shard_map/convert_element_type | solution.py:82
  603.7 4.8 divide_convert_fusion
  608.5 1.6 copy-done.9
  610.6 2.9 convolution_convert_fusion
  (53 shorter events, 11.1 us)
Async XLA Ops:
  7.2 1.9 copy-start.11
  7.2 3.3 copy-start.14
  7.2 509.9 %all-gather.2.cloned.1.call-start = ((), (), s32[]{:S(2)}) async-start(), calls=%async_computation | async-start | bytes 106954752 | tf_op jit(solution)/shard_map/all_gather | solution.py:63
  7.2 3.4 copy-start.10
  7.2 3.3 copy-start.16
  11.1 1.0 copy-start.12
  30.0 1.2 copy-start.7
  31.8 12.6 %copy-start.1 = (bf16[8,256,256]{1,2,0:T(8,128)(2,1)}, bf16[8,256,256]{1,2,0:T(8,128)(2,1)S(1)}, u32[]{:S(2)}) copy-start(bf16[8,256,256]{1,2,0:T(8,128)(2,1)S(1)} %copy.53) | copy-start | bytes 3145732
  32.3 12.1 %copy-start.3 = (bf16[8,256,256]{1,2,0:T(8,128)(2,1)}, bf16[8,256,256]{1,2,0:T(8,128)(2,1)S(1)}, u32[]{:S(2)}) copy-start(bf16[8,256,256]{1,2,0:T(8,128)(2,1)S(1)} %copy.54) | copy-start | bytes 3145732
  34.2 10.2 %copy-start.5 = (bf16[8,256,256]{1,2,0:T(8,128)(2,1)}, bf16[8,256,256]{1,2,0:T(8,128)(2,1)S(1)}, u32[]{:S(2)}) copy-start(bf16[8,256,256]{1,2,0:T(8,128)(2,1)S(1)} %copy.55) | copy-start | bytes 3145732
  44.4 1.7 copy-start.8
  44.4 1.7 copy-start.15
  550.6 4.6 copy-start
  597.0 6.7 %copy-start.2 = (bf16[8,256,256]{1,2,0:T(8,128)(2,1)S(1)}, bf16[8,256,256]{1,2,0:T(8,128)(2,1)}, u32[]{:S(2)}) copy-start(bf16[8,256,256]{1,2,0:T(8,128)(2,1)} %copy-done.1) | copy-start | bytes 3145732
  597.0 6.7 %copy-start.4 = (bf16[8,256,256]{1,2,0:T(8,128)(2,1)S(1)}, bf16[8,256,256]{1,2,0:T(8,128)(2,1)}, u32[]{:S(2)}) copy-start(bf16[8,256,256]{1,2,0:T(8,128)(2,1)} %copy-done.3) | copy-start | bytes 3145732
  597.0 6.7 %copy-start.6 = (bf16[8,256,256]{1,2,0:T(8,128)(2,1)S(1)}, bf16[8,256,256]{1,2,0:T(8,128)(2,1)}, u32[]{:S(2)}) copy-start(bf16[8,256,256]{1,2,0:T(8,128)(2,1)} %copy-done.5) | copy-start | bytes 3145732
  603.7 6.4 %copy-start.13 = (bf16[256,2048]{1,0:T(8,128)(2,1)S(1)}, bf16[256,2048]{1,0:T(8,128)(2,1)}, u32[]{:S(2)}) copy-start(bf16[256,2048]{1,0:T(8,128)(2,1)} %param.16) | copy-start | bytes 3145732
  608.5 1.6 copy-start.9
Sparse Core Ops, SparseCore 0:
  30.2 486.8 all-gather.1
